TPU v7x, 32 devices: a whole 2x2x4 slice. The times are simulated.
32 devices in a mesh: sample: 2 (over y), harm: 16 (over z, x, core).
Axes of the slice: x: 2, y: 2, z: 4, core: 2. Of those that a mesh axis runs over, the one named last changes fastest.
Arguments:
- inputs: bfloat16 [128, 64, 512], P('sample', 'harm'), parts along dimension 0, may hold values from -6 to 6
- col_list: int32 [128], P('sample'), parts along dimension 0, may hold values from 0 to 63, each once
- row_list: int32 [128], P('sample'), parts along dimension 0, may hold values from 0 to 63, each once
- gain_attn: float32 [512], replicated, may hold values from 0.25 to 1.75
- w_qkv: bfloat16 [512, 1536], replicated
- w_out: bfloat16 [512, 512], replicated, may hold values from -0.25 to 0.25
- gain_ffn: float32 [512], replicated, may hold values from 0.25 to 1.75
- w_gate: bfloat16 [512, 1024], P('harm'), may hold values from -0.25 to 0.25
- w_up: bfloat16 [512, 1024], P('harm'), may hold values from -0.25 to 0.25
- w_down: bfloat16 [1024, 512], P('harm'), may hold values from -0.1875 to 0.1875
Outputs:
- result: bfloat16 [64, 128, 512], P('harm', 'sample'), parts along dimension 1
There are 2 independent parts, one for each index of `sample`. A program takes and returns all parts, laid end to end along the dimension named above; an argument that names none is the same for every part. Nothing has to cross between parts.
Inputs may be any that keep to these rules, and one draw needn't show every extreme that they name: col_list names every order m of 0 to 63 exactly once. row_list names every degree ell of 0 to 63 exactly once.
All inputs are finite; a program needn't handle non-finite values.
Results may differ from a plain program's by a relative error of at most 0.0073.
Values may be sent and summed in bfloat16 or wider, within the bound.
A program may use at most 64 MiB of HBM per device.

v0:
```python
import jax
import jax.numpy as jnp
from jax import lax
from jax.sharding import PartitionSpec as P

HEADS = 8
WIN = 256


eps = 1e-06
masked = -1e30


def rms_scale(values, gain):
    values = values.astype(jnp.float32)
    mean_sq = jnp.mean(values * values, axis=-1, keepdims=True)
    return values * lax.rsqrt(mean_sq + eps) * gain


def split_heads(block, start, split, head_dim):
    piece = block[..., start : start + split]
    return piece.reshape(piece.shape[:-1] + (split // head_dim, head_dim))


def softmax_rounded(scores):
    top = jnp.max(scores, axis=-1, keepdims=True)
    weights = jnp.exp(scores - top)
    return (weights / jnp.sum(weights, axis=-1, keepdims=True)).astype(jnp.bfloat16)


def column_attention(query, keys, values, starts, scale):
    length = query.shape[0]
    here = jnp.arange(length, dtype=jnp.int32)
    offset = here[None, :] - here[:, None]
    band = (offset >= -(WIN // 2)) & (offset < WIN // 2)
    allowed = band[None] & (here[None, None, :] >= starts[:, None, None])
    scores = jnp.einsum("lchd,kchd->chlk", query, keys, preferred_element_type=jnp.float32) * scale
    scores = jnp.where(allowed[:, None], scores, masked)
    probs = softmax_rounded(scores)
    mixed = jnp.einsum("chlk,kchd->lchd", probs, values, preferred_element_type=jnp.float32)
    return mixed.astype(jnp.bfloat16)


def row_attention(query, keys, values, marks, limits, scale):
    diff = marks[None, :] - marks[:, None]
    band = (diff >= -(WIN // 2)) & (diff < WIN // 2)
    allowed = band[None] & (marks[None, None, :] <= limits[:, None, None])
    scores = jnp.einsum("ishd,ithd->ihst", query, keys, preferred_element_type=jnp.float32) * scale
    scores = jnp.where(allowed[:, None], scores, masked)
    probs = softmax_rounded(scores)
    mixed = jnp.einsum("ihst,ithd->ishd", probs, values, preferred_element_type=jnp.float32)
    return mixed.astype(jnp.bfloat16)


def per_device(inputs, col_list, row_list, gain_attn, w_qkv, w_out, gain_ffn, w_gate, w_up, w_down):
    place = lax.axis_index("harm")
    groups = lax.axis_size("harm")
    length, cols, width = inputs.shape
    rows_here = length // groups
    head_dim = width // HEADS
    half = HEADS // 2
    split = half * head_dim
    scale = head_dim ** (-0.5)
    my_cols = lax.dynamic_slice_in_dim(col_list, place * cols, cols)
    my_rows = lax.dynamic_slice_in_dim(row_list, place * rows_here, rows_here)
    gate_full, up_full, down_full = (
        lax.all_gather(w_gate, "harm", axis=0, tiled=True),
        lax.all_gather(w_up, "harm", axis=0, tiled=True),
        lax.all_gather(w_down, "harm", axis=0, tiled=True),
    )
    normed = rms_scale(inputs, gain_attn).astype(jnp.bfloat16)
    flat = normed.reshape(length * cols, width)
    qkv = jnp.dot(flat, w_qkv, preferred_element_type=jnp.float32)
    qkv = qkv.astype(jnp.bfloat16).reshape(length, cols, 3 * width)
    a_ell = column_attention(
        split_heads(qkv, 0, split, head_dim),
        split_heads(qkv, width, split, head_dim),
        split_heads(qkv, 2 * width, split, head_dim),
        my_cols,
        scale,
    )
    a_ell = a_ell.reshape(length, cols, split)
    feat_rows = jnp.take(inputs, row_list, axis=0)
    ell_rows = jnp.take(a_ell, row_list, axis=0)
    query_rows = jnp.take(qkv[:, :, split:width], row_list, axis=0)
    key_rows = jnp.take(qkv[:, :, width + split : 2 * width], row_list, axis=0)
    value_rows = jnp.take(qkv[:, :, 2 * width + split :], row_list, axis=0)
    feat_here, ell_here, query_here, key_here, value_here = (
        lax.all_to_all(feat_rows, "harm", split_axis=0, concat_axis=1, tiled=True),
        lax.all_to_all(ell_rows, "harm", split_axis=0, concat_axis=1, tiled=True),
        lax.all_to_all(query_rows, "harm", split_axis=0, concat_axis=1, tiled=True),
        lax.all_to_all(key_rows, "harm", split_axis=0, concat_axis=1, tiled=True),
        lax.all_to_all(value_rows, "harm", split_axis=0, concat_axis=1, tiled=True),
    )
    shape_heads = (rows_here, length, half, head_dim)
    a_m = row_attention(
        query_here.reshape(shape_heads),
        key_here.reshape(shape_heads),
        value_here.reshape(shape_heads),
        col_list,
        my_rows,
        scale,
    )
    attn = jnp.concatenate([ell_here, a_m.reshape(rows_here, length, split)], axis=-1)
    tokens = rows_here * length
    resid = feat_here.astype(jnp.float32).reshape(tokens, width) + jnp.dot(
        attn.reshape(tokens, width), w_out, preferred_element_type=jnp.float32
    )
    normed_ffn = rms_scale(resid, gain_ffn).astype(jnp.bfloat16)
    gate = jnp.dot(normed_ffn, gate_full, preferred_element_type=jnp.float32)
    up = jnp.dot(normed_ffn, up_full, preferred_element_type=jnp.float32)
    hidden = (jax.nn.silu(gate) * up).astype(jnp.bfloat16)
    final = (resid + jnp.dot(hidden, down_full, preferred_element_type=jnp.float32)).reshape(
        rows_here, length, width
    )
    valid = col_list[None, :] <= my_rows[:, None]
    return jnp.where(valid[:, :, None], final, 0.0).astype(jnp.bfloat16)


def solution(mesh):
    placed = (
        P("sample", "harm", None),
        P("sample"),
        P("sample"),
        P(),
        P(),
        P(),
        P(),
        P("harm", None),
        P("harm", None),
        P("harm", None),
    )
    return jax.shard_map(
        per_device, mesh=mesh, in_specs=placed, out_specs=P("harm", "sample", None), check_vma=False
    )
```

profile of v0, /device:TPU:1, one launch (start us, length us, event | category | flops | bytes accessed | tf_op | source)
XLA Modules:
  0.0 140.8 jit_solution(10194991990076802420)
XLA Ops:
  6.5 0.0 copy-start
  6.5 0.0 all-gather.4.cloned.1.call-start
  6.5 0.7 all-gather.4.cloned.1.call-update
  7.3 0.0 all-gather.6.cloned.1.call-start
  7.3 0.7 all-gather.6.cloned.1.call-update
  8.0 0.7 dynamic_slice.7
  8.8 0.1 iota_compare_fusion
  8.8 1.2 fusion.15
  10.0 1.2 fusion.17
  11.2 0.1 reshape.198
  11.3 0.6 convolution_convert_fusion
  11.8 0.2 reshape.199
  12.0 0.3 fusion.44
  12.3 0.1 broadcast_and_fusion.1
  12.4 0.2 reshape.263
  12.6 0.2 reshape.264
  12.8 0.2 copy.68
  13.0 0.3 fusion.8
  13.3 0.1 fusion.45
  13.4 0.0 copy-start.4
  13.4 0.3 convolution_convert_fusion.2
  13.7 0.2 copy.74
  13.9 0.2 copy-done.4
  14.1 0.7 gather_fusion.1
  14.8 0.0 copy-start.1
  14.8 0.7 gather_fusion.2
  15.5 0.7 gather_fusion.3
  16.2 0.7 gather_fusion.4
  16.9 1.1 broadcast_select_fusion.4
  18.0 14.2 %all_to_all.69 = bf16[64,4,256]{2,1,0:T(4,128)(2,1)S(1)} all-to-all(bf16[64,4,256]{2,1,0:T(4,128)(2,1)S(1)} %get-tuple-element.14), channel_id=1, replica_groups=mesh['sample'=2,'harm'=16] {'harm'}, dimensions={0} | all-to-all | bytes 262144 | tf_op jit(solution)/shard_map/all_to_all | solution.py:91
  32.2 4.6 %all-to-all-start.4 = ((bf16[64,4,256]{2,1,0:T(4,128)(2,1)}), bf16[64,4,256]{2,1,0:T(4,128)(2,1)S(1)}, u32[]{:S(2)}, u32[]{:S(2)}) async-start(bf16[64,4,256]{2,1,0:T(4,128)(2,1)} %get-tuple-element.15), calls=%async_computation.4 | async-start | bytes 262144 | tf_op jit(solution)/shard_map/all_to_all | solution.py:92
  36.8 0.0 all-gather.8.cloned.1.call-start
  36.9 0.7 all-gather.8.cloned.1.call-update
  37.6 0.1 dynamic_slice.6
  37.6 7.7 %all-to-all-done.4 = bf16[64,4,256]{2,1,0:T(4,128)(2,1)S(1)} async-done(((bf16[64,4,256]{2,1,0:T(4,128)(2,1)}), bf16[64,4,256]{2,1,0:T(4,128)(2,1)S(1)}, u32[]{:S(2)}, u32[]{:S(2)}) %all-to-all-start.4) | async-done | bytes 131104 | tf_op jit(solution)/shard_map/all_to_all | solution.py:92
  45.3 3.9 %all-to-all-start.2 = ((bf16[64,4,256]{2,1,0:T(4,128)(2,1)}), bf16[64,4,256]{2,1,0:T(4,128)(2,1)S(1)}, u32[]{:S(2)}, u32[]{:S(2)}) async-start(bf16[64,4,256]{2,1,0:T(4,128)(2,1)} %get-tuple-element.13), calls=%async_computation.2 | async-start | bytes 262144 | tf_op jit(solution)/shard_map/all_to_all | solution.py:93
  49.2 0.1 broadcast_compare_fusion
  49.3 0.1 fusion.39
  49.4 6.8 %all-to-all-done.2 = bf16[64,4,256]{2,1,0:T(4,128)(2,1)S(1)} async-done(((bf16[64,4,256]{2,1,0:T(4,128)(2,1)}), bf16[64,4,256]{2,1,0:T(4,128)(2,1)S(1)}, u32[]{:S(2)}, u32[]{:S(2)}) %all-to-all-start.2) | async-done | bytes 131104 | tf_op jit(solution)/shard_map/all_to_all | solution.py:93
  56.2 4.5 %all-to-all-start.1 = ((bf16[64,4,256]{2,1,0:T(4,128)(2,1)}), bf16[64,4,256]{2,1,0:T(4,128)(2,1)S(1)}, u32[]{:S(2)}, u32[]{:S(2)}) async-start(bf16[64,4,256]{2,1,0:T(4,128)(2,1)} %get-tuple-element.12), calls=%async_computation.1 | async-start | bytes 262144 | tf_op jit(solution)/shard_map/all_to_all | solution.py:90
  60.7 0.1 broadcast_and_fusion
  60.8 0.8 gather_fusion
  61.6 0.9 broadcast_select_fusion
  62.5 0.2 reshape.205
  62.8 0.2 reshape.206
  62.9 6.3 %all-to-all-done.1 = bf16[64,4,256]{2,1,0:T(4,128)(2,1)S(1)} async-done(((bf16[64,4,256]{2,1,0:T(4,128)(2,1)}), bf16[64,4,256]{2,1,0:T(4,128)(2,1)S(1)}, u32[]{:S(2)}, u32[]{:S(2)}) %all-to-all-start.1) | async-done | bytes 131104 | tf_op jit(solution)/shard_map/all_to_all | solution.py:90
  69.2 3.7 %all-to-all-start = ((bf16[64,4,512]{2,1,0:T(4,128)(2,1)}), bf16[64,4,512]{2,1,0:T(4,128)(2,1)S(1)}, u32[]{:S(2)}, u32[]{:S(2)}) async-start(bf16[64,4,512]{2,1,0:T(4,128)(2,1)} %broadcast_select_fusion), calls=%async_computation | async-start | bytes 524288 | tf_op jit(solution)/shard_map/all_to_all | solution.py:89
  73.0 0.3 fusion.7
  73.3 0.2 reshape.204
  73.5 0.1 fusion.46
  73.6 0.3 fusion.9
  73.9 0.2 copy.83
  74.1 0.2 concatenate.9
  74.4 8.9 %all-to-all-done = bf16[64,4,512]{2,1,0:T(4,128)(2,1)S(1)} async-done(((bf16[64,4,512]{2,1,0:T(4,128)(2,1)}), bf16[64,4,512]{2,1,0:T(4,128)(2,1)S(1)}, u32[]{:S(2)}, u32[]{:S(2)}) %all-to-all-start) | async-done | bytes 262176 | tf_op jit(solution)/shard_map/all_to_all | solution.py:89
  83.4 0.0 copy-start.3
  83.4 0.2 reshape.208
  83.6 1.4 %multiply_reduce_fusion = (f32[256]{0:T(256)S(1)}, f32[256,512]{1,0:T(8,128)S(1)}) fusion(f32[256,512]{1,0:T(8,128)S(1)} %reshape.208, bf16[512,512]{1,0:T(8,128)(2,1)} %param.17, bf16[256,256]{1,0:T(8,128)(2,1)S(1)} %concatenate.9, bf16[256,256]{1,0:T(8,128)(2,1)S(1)} %concatenate.8), kind=kOutput, calls=%fused_computation.37 | convolution fusion | flops 135134976 | bytes 1836032 | tf_op jit(solution)/shard_map/dot_general | solution.py:106
  85.1 0.0 all-gather.4.cloned.1.call-done
  85.1 0.0 copy-done.3
  85.1 1.7 %fusion.19 = f32[256,1024]{1,0:T(8,128)S(1)} fusion(bf16[512,1024]{1,0:T(8,128)(2,1)} %all-gather.4.cloned.1.call-done, f32[256,512]{1,0:T(8,128)S(1)} %get-tuple-element.17, f32[512]{0:T(512)S(1)} %copy-done.3, f32[256]{0:T(256)S(1)} %add_rsqrt_fusion.1), kind=kOutput, calls=%fused_computation.40 | convolution fusion | flops 268828672 | bytes 2624512 | tf_op jit(solution)/shard_map/dot_general | solution.py:110
  86.8 5.0 %all-gather.6.cloned.1.call-done = bf16[512,1024]{1,0:T(8,128)(2,1)} async-done(((bf16[32,1024]{1,0:T(8,128)(2,1)}), bf16[512,1024]{1,0:T(8,128)(2,1)}) %all-gather.6.cloned.1.call-update) | async-done | bytes 1048592 | tf_op jit(solution)/shard_map/all_gather | solution.py:68
  91.9 39.2 %all-gather.8.cloned.1.call-done = bf16[1024,512]{1,0:T(8,128)(2,1)} async-done(((bf16[64,512]{1,0:T(8,128)(2,1)}), bf16[1024,512]{1,0:T(8,128)(2,1)}) %all-gather.8.cloned.1.call-update) | async-done | bytes 1048592 | tf_op jit(solution)/shard_map/all_gather | solution.py:69
  131.1 2.4 %convolution_add_fusion = bf16[256,512]{1,0:T(8,128)(2,1)S(1)} fusion(f32[256,512]{1,0:T(8,128)S(1)} %get-tuple-element.17, bf16[1024,512]{1,0:T(8,128)(2,1)} %all-gather.8.cloned.1.call-done, bf16[512,1024]{1,0:T(8,128)(2,1)} %all-gather.6.cloned.1.call-done, f32[256,1024]{1,0:T(8,128)S(1)} %fusion.19, f32[512]{0:T(512)S(1)} %copy-done.3, ...), kind=kOutput, calls=%fused_computation.12 | convolution fusion | flops 539099136 | bytes 3935232 | tf_op jit(solution)/shard_map/dot_general | solution.py:113
  133.5 0.8 select_convert_fusion
  (16 shorter events, 0.3 us)
Async XLA Ops:
  6.5 4.7 %copy-start = (bf16[512,1536]{1,0:T(8,128)(2,1)S(1)}, bf16[512,1536]{1,0:T(8,128)(2,1)}, u32[]{:S(2)}) copy-start(bf16[512,1536]{1,0:T(8,128)(2,1)} %param.16) | copy-start | bytes 4718596
  6.5 78.5 %all-gather.4.cloned.1.call-start = ((), (), s32[]{:S(2)}) async-start(), calls=%async_computation.5 | async-start | bytes 1114112 | tf_op jit(solution)/shard_map/all_gather | solution.py:67
  7.3 84.6 %all-gather.6.cloned.1.call-start = ((), (), s32[]{:S(2)}) async-start(), calls=%async_computation.6 | async-start | bytes 1114112 | tf_op jit(solution)/shard_map/all_gather | solution.py:68
  13.4 0.7 copy-start.4
  14.1 35.2 %copy-start.2 = (s32[64]{0:T(128)S(1)}, s32[64]{0:T(128)}, u32[]{:S(2)}) copy-start(s32[64]{0:T(128)} %param.13) | copy-start | bytes 772
  14.8 46.0 %copy-start.1 = (bf16[64,4,512]{2,1,0:T(4,128)(2,1)S(1)}, bf16[64,4,512]{2,1,0:T(4,128)(2,1)}, u32[]{:S(2)}) copy-start(bf16[64,4,512]{2,1,0:T(4,128)(2,1)} %param.12) | copy-start | bytes 786436
  32.2 13.2 %all-to-all-start.4 = ((bf16[64,4,256]{2,1,0:T(4,128)(2,1)}), bf16[64,4,256]{2,1,0:T(4,128)(2,1)S(1)}, u32[]{:S(2)}, u32[]{:S(2)}) async-start(bf16[64,4,256]{2,1,0:T(4,128)(2,1)} %get-tuple-element.15), calls=%async_computation.4 | async-start | bytes 262144 | tf_op jit(solution)/shard_map/all_to_all | solution.py:92
  36.8 94.2 %all-gather.8.cloned.1.call-start = ((), (), s32[]{:S(2)}) async-start(), calls=%async_computation.7 | async-start | bytes 1114112 | tf_op jit(solution)/shard_map/all_gather | solution.py:69
  45.3 10.8 %all-to-all-start.2 = ((bf16[64,4,256]{2,1,0:T(4,128)(2,1)}), bf16[64,4,256]{2,1,0:T(4,128)(2,1)S(1)}, u32[]{:S(2)}, u32[]{:S(2)}) async-start(bf16[64,4,256]{2,1,0:T(4,128)(2,1)} %get-tuple-element.13), calls=%async_computation.2 | async-start | bytes 262144 | tf_op jit(solution)/shard_map/all_to_all | solution.py:93
  56.2 13.0 %all-to-all-start.1 = ((bf16[64,4,256]{2,1,0:T(4,128)(2,1)}), bf16[64,4,256]{2,1,0:T(4,128)(2,1)S(1)}, u32[]{:S(2)}, u32[]{:S(2)}) async-start(bf16[64,4,256]{2,1,0:T(4,128)(2,1)} %get-tuple-element.12), calls=%async_computation.1 | async-start | bytes 262144 | tf_op jit(solution)/shard_map/all_to_all | solution.py:90
  69.2 14.1 %all-to-all-start = ((bf16[64,4,512]{2,1,0:T(4,128)(2,1)}), bf16[64,4,512]{2,1,0:T(4,128)(2,1)S(1)}, u32[]{:S(2)}, u32[]{:S(2)}) async-start(bf16[64,4,512]{2,1,0:T(4,128)(2,1)} %broadcast_select_fusion), calls=%async_computation | async-start | bytes 524288 | tf_op jit(solution)/shard_map/all_to_all | solution.py:89
  83.4 1.7 %copy-start.3 = (f32[512]{0:T(512)S(1)}, f32[512]{0:T(512)}, u32[]{:S(2)}) copy-start(f32[512]{0:T(512)} %param.18) | copy-start | bytes 6148
Sparse Core Ops, SparseCore 0:
  9.5 42.0 all-gather.3
  53.8 38.0 all-gather.5
  94.0 36.9 all-gather.7
where the time goes:
time: 142 us; the launch traced here: 141 us
  waiting for transfers between devices  76.1 us (54%)
  starting transfers between devices  16.8 us (12%)
  blocking collectives  14.2 us (10%)
  between operations  13.4 us (9%)
  matrix products  7.23 us (5%)
  local copies, waits for them, and re-layouts  7.2 us (5%)
  other arithmetic  5.9 us (4%)
    all_gather x1, waiting for transfers between devices, per_device(): lax.all_gather(w_down, 'harm', axis=0, tiled=True)  39.2 us
    all_to_all x1, blocking collectives, per_device(): lax.all_to_all(query_rows, 'harm', split_axis=0, concat_axis=1, tiled=True)  14.2 us
    all_to_all x1, waiting for transfers between devices, per_device(): lax.all_to_all(feat_rows, 'harm', split_axis=0, concat_axis=1, tiled=True)  8.93 us
    all_to_all x1, waiting for transfers between devices, per_device(): lax.all_to_all(key_rows, 'harm', split_axis=0, concat_axis=1, tiled=True)  7.71 us
    all_to_all x1, waiting for transfers between devices, per_device(): lax.all_to_all(value_rows, 'harm', split_axis=0, concat_axis=1, tiled=True)  6.79 us
    all_to_all x1, waiting for transfers between devices, per_device(): lax.all_to_all(ell_rows, 'harm', split_axis=0, concat_axis=1, tiled=True)  6.29 us
    all_gather x1, waiting for transfers between devices, per_device(): lax.all_gather(w_up, 'harm', axis=0, tiled=True)  5.04 us
    all_to_all x1, starting transfers between devices, per_device(): lax.all_to_all(key_rows, 'harm', split_axis=0, concat_axis=1, tiled=True)  4.64 us
  transfers between devices with their start and end apart: 7, of which 6 were waited for; matrix products, arithmetic and copies ran while one was open for 12% of the time, Pallas kernels for 0%

commit v1 on v0

v1 whole, which is shorter than its diff:
```python
import functools

import jax
import jax.numpy as jnp
from jax import lax
from jax.experimental import pallas as pl
from jax.experimental.pallas import tpu as pltpu
from jax.sharding import PartitionSpec as P

HEADS = 8
WIN = 256
MESH = pl.DeviceIdType.MESH

eps = 1e-06
masked = -1e30


def rms_scale(values, gain):
    values = values.astype(jnp.float32)
    mean_sq = jnp.mean(values * values, axis=-1, keepdims=True)
    return values * lax.rsqrt(mean_sq + eps) * gain


def dot(a, b):
    return jnp.dot(a, b, preferred_element_type=jnp.float32)


def one_hot_rows(index, size):
    lanes = lax.broadcasted_iota(jnp.int32, (index.shape[0], size), 1)
    return jnp.where(lanes == index, 1.0, 0.0).astype(jnp.bfloat16)


def attention(query, key_ref, value_ref, start, width, allowed, scale, pair):
    low = lax.broadcasted_iota(jnp.int32, query.shape, 1) < pair // 2
    keys = key_ref[:, start : start + width]
    values = value_ref[:, start : start + width]
    zero = jnp.zeros_like(query)
    mixed = []
    for part in (jnp.where(low, query, zero), jnp.where(low, zero, query)):
        scores = lax.dot_general(part, keys, (((1,), (1,)), ((), ())), preferred_element_type=jnp.float32)
        scores = jnp.where(allowed, scores * scale, masked)
        top = jnp.max(scores, axis=-1, keepdims=True)
        weights = jnp.exp(scores - top)
        probs = (weights / jnp.sum(weights, axis=-1, keepdims=True)).astype(jnp.bfloat16)
        mixed.append(dot(probs, values))
    return jnp.where(low, mixed[0], mixed[1]).astype(jnp.bfloat16)


def kernel(
    n, x_ref, mc_ref, mr_ref, gain_a_ref, w_qkv_ref, w_out_ref, gain_f_ref, gate_ref, up_ref, down_ref,
    out_ref, sent, ell_out, q_buf, k_buf, v_buf, got, got_ell, attn_m, gu, dn,
    sx_send, sx_recv, sa_send, sa_recv, z_send, z_recv, x_send, x_recv, c_send, c_recv,
):
    me = lax.axis_index("harm")
    outer = n // 4
    zc, inner = me // 4, me % 4
    side, core = inner // 2, inner % 2
    other_side = zc * 4 + (1 - side) * 2 + core
    other_core = zc * 4 + side * 2 + (1 - core)
    depth = gate_ref.shape[0]
    deep = down_ref.shape[0]
    tokens, width = x_ref.shape
    block = tokens // n
    split = width // 2
    head_dim = width // HEADS
    pair = 2 * head_dim
    scale = head_dim ** (-0.5)
    step = min(tokens, 256)

    barrier = pltpu.get_barrier_semaphore()
    for d in range(1, n):
        pl.semaphore_signal(barrier, inc=1, device_id={"harm": (me + d) % n}, device_id_type=MESH)

    gu[0, pl.ds(pl.multiple_of(me * depth, depth), depth), :] = gate_ref[...]
    gu[1, pl.ds(pl.multiple_of(me * depth, depth), depth), :] = up_ref[...]
    dn[pl.ds(pl.multiple_of(me * deep, deep), deep), :] = down_ref[...]
    sent[...] = dot(one_hot_rows(mc_ref[:, 0:1], tokens), x_ref[...]).astype(jnp.bfloat16)

    pl.semaphore_wait(barrier, n - 1)

    def rows_of(ref, i):
        return ref.at[pl.ds(pl.multiple_of(i * block, block), block), :]

    def to_row(src, dst, send, recv, d):
        peer = (me + d) % n
        return pltpu.make_async_remote_copy(
            src_ref=rows_of(src, peer), dst_ref=rows_of(dst, me), send_sem=send.at[d], recv_sem=recv.at[d],
            device_id={"harm": peer}, device_id_type=MESH,
        )

    def shard(i, send, recv, slot, device):
        first = gu.at[:, pl.ds(pl.multiple_of(i * depth, depth), depth), :]
        second = dn.at[pl.ds(pl.multiple_of(i * deep, deep), deep), :]
        return [
            pltpu.make_async_remote_copy(
                src_ref=ref, dst_ref=ref, send_sem=send.at[slot, k], recv_sem=recv.at[slot, k],
                device_id={"harm": device}, device_id_type=MESH,
            )
            for k, ref in enumerate((first, second))
        ]

    def place(d, s, c):
        return ((zc + outer - d) % outer) * 4 + s * 2 + c

    pending = []

    def start(copies):
        for copy in copies:
            copy.start()
        pending.extend(copies)

    start([to_row(sent, got, sx_send, sx_recv, d) for d in range(1, n)])
    for d in range(1, outer):
        start(shard(me, z_send, z_recv, d, ((zc + d) % outer) * 4 + inner))
    start(shard(me, x_send, x_recv, 0, other_side))
    start(shard(me, c_send, c_recv, 0, other_core))
    rows_of(got, me)[...] = rows_of(sent, me)[...]

    def project(source, first):
        normed = rms_scale(source[...], gain_a_ref[...]).astype(jnp.bfloat16)
        for buf, base in ((q_buf, 0), (k_buf, width), (v_buf, 2 * width)):
            buf[...] = dot(normed, w_qkv_ref[:, base + first : base + first + split]).astype(jnp.bfloat16)

    def attend(dest, marks, level, along_ell):
        def body(i, carry):
            rows = pl.ds(pl.multiple_of(i * step, step), step)
            ell_q, col_q = mc_ref[rows, level : level + 1], mc_ref[rows, marks : marks + 1]
            ell_k, col_k = mr_ref[level : level + 1, :], mr_ref[marks : marks + 1, :]
            if along_ell:
                same, diff = col_q == col_k, ell_k - ell_q
            else:
                same, diff = ell_q == ell_k, col_k - col_q
            allowed = same & (diff >= -(WIN // 2)) & (diff < WIN // 2) & (ell_k >= col_k)
            for p in range(split // pair):
                query = q_buf[rows, p * pair : (p + 1) * pair]
                dest[rows, p * pair : (p + 1) * pair] = attention(
                    query, k_buf, v_buf, p * pair, pair, allowed, scale, pair
                )
            return carry

        lax.fori_loop(0, tokens // step, body, 0)

    project(sent, 0)
    attend(ell_out, 2, 1, True)
    start([to_row(ell_out, got_ell, sa_send, sa_recv, d) for d in range(1, n)])
    rows_of(got_ell, me)[...] = rows_of(ell_out, me)[...]

    for d in range(1, outer):
        i = place(d, side, core)
        for copy in shard(i, z_send, z_recv, d, me):
            copy.wait_recv()
        start(shard(i, x_send, x_recv, d, other_side))
        start(shard(i, c_send, c_recv, d, other_core))

    for d in range(1, n):
        to_row(sent, got, sx_send, sx_recv, d).wait_recv()
    project(got, split)
    attend(attn_m, 4, 3, False)

    for d in range(outer):
        i = place(d, 1 - side, core)
        for copy in shard(i, x_send, x_recv, d, me):
            copy.wait_recv()
        start(shard(i, c_send, c_recv, outer + d, other_core))

    for d in range(1, n):
        to_row(ell_out, got_ell, sa_send, sa_recv, d).wait_recv()
    resid = got[...].astype(jnp.float32) + (
        dot(got_ell[...], w_out_ref[:split, :]) + dot(attn_m[...], w_out_ref[split:, :])
    )
    normed_ffn = rms_scale(resid, gain_f_ref[...]).astype(jnp.bfloat16)

    for slot in range(2 * outer):
        i = place(slot % outer, side if slot < outer else 1 - side, 1 - core)
        for copy in shard(i, c_send, c_recv, slot, me):
            copy.wait_recv()
    gate = dot(normed_ffn, gu[0])
    up = dot(normed_ffn, gu[1])
    hidden = (gate / (1.0 + jnp.exp(-gate)) * up).astype(jnp.bfloat16)
    final = resid + dot(hidden, dn[...])
    valid = mc_ref[:, 4:5] <= mc_ref[:, 3:4]
    final = jnp.where(valid, final, 0.0).astype(jnp.bfloat16)
    out_ref[...] = dot(one_hot_rows(mc_ref[:, 5:6], tokens), final).astype(jnp.bfloat16)
    for copy in pending:
        copy.wait_send()


def per_device(n, inputs, col_list, row_list, gain_attn, w_qkv, w_out, gain_ffn, w_gate, w_up, w_down):
    place = lax.axis_index("harm")
    length, cols, width = inputs.shape
    rows_here = length // n
    tokens = length * cols
    split = width // 2
    my_cols = lax.dynamic_slice_in_dim(col_list, place * cols, cols)
    my_rows = lax.dynamic_slice_in_dim(row_list, place * rows_here, rows_here)
    before, after = (length, cols), (n, rows_here, cols)
    slot = jnp.arange(cols, dtype=jnp.int32)
    order = jnp.arange(tokens, dtype=jnp.int32).reshape(n, rows_here, cols).transpose(0, 1, 2)
    back = order.transpose(1, 0, 2)
    table = [
        jnp.broadcast_to(row_list[:, None] * cols + slot[None, :], before),
        jnp.broadcast_to(row_list[:, None], before),
        jnp.broadcast_to(my_cols[None, :], before),
        jnp.broadcast_to(my_rows[None, :, None], after),
        jnp.broadcast_to(col_list.reshape(n, 1, cols), after),
        back,
        back,
        back,
    ]
    by_row = jnp.stack([entry.reshape(tokens) for entry in table], axis=0)
    by_col = by_row.T
    bf16, f32 = jnp.bfloat16, jnp.float32
    depth, ff = w_gate.shape
    deep = w_down.shape[0]
    outer = n // 4
    vmem = pl.BlockSpec(memory_space=pltpu.VMEM)
    dma = pltpu.SemaphoreType.DMA
    result = pl.pallas_call(
        functools.partial(kernel, n),
        out_shape=jax.ShapeDtypeStruct((tokens, width), bf16),
        in_specs=[vmem] * 10,
        out_specs=vmem,
        scratch_shapes=[
            pltpu.VMEM((tokens, width), bf16),
            pltpu.VMEM((tokens, split), bf16),
            pltpu.VMEM((tokens, split), bf16),
            pltpu.VMEM((tokens, split), bf16),
            pltpu.VMEM((tokens, split), bf16),
            pltpu.VMEM((tokens, width), bf16),
            pltpu.VMEM((tokens, split), bf16),
            pltpu.VMEM((tokens, split), bf16),
            pltpu.VMEM((2, depth * n, ff), bf16),
            pltpu.VMEM((deep * n, width), bf16),
            dma((n,)), dma((n,)), dma((n,)), dma((n,)),
            dma((outer, 2)), dma((outer, 2)),
            dma((outer, 2)), dma((outer, 2)),
            dma((2 * outer, 2)), dma((2 * outer, 2)),
        ],
        compiler_params=pltpu.CompilerParams(
            collective_id=0, has_side_effects=True, vmem_limit_bytes=56 * 1024 * 1024
        ),
    )(
        inputs.reshape(tokens, width), by_col, by_row, gain_attn.reshape(1, width), w_qkv, w_out,
        gain_ffn.reshape(1, width), w_gate, w_up, w_down,
    )
    return result.reshape(rows_here, length, width)


def solution(mesh):
    placed = (
        P("sample", "harm", None),
        P("sample"),
        P("sample"),
        P(),
        P(),
        P(),
        P(),
        P("harm", None),
        P("harm", None),
        P("harm", None),
    )
    return jax.shard_map(
        functools.partial(per_device, mesh.shape["harm"]),
        mesh=mesh, in_specs=placed, out_specs=P("harm", "sample", None), check_vma=False,
    )
```

time: 142 us -> 53.8 us (0.38)
  the two profiles are of different devices: /device:TPU:1 before, /device:TPU:25 now
where the time goes in v1:
time: 53.8 us; the launch traced here: 53.6 us
  Pallas kernels  44.9 us (83%)
  local copies, waits for them, and re-layouts  7.87 us (15%)
  other arithmetic  0.74 us (1%)
    pallas_call x1, Pallas kernels, per_device(): pl.pallas_call(functools.partial(kernel, n), out_shape=jax.ShapeDtypeStru...  44.9 us
    reshape x1, local copies, waits for them, and re-layouts, per_device(): inputs.reshape(tokens, width)  1.72 us
    unnamed x3, local copies, waits for them, and re-layouts  1.67 us

profile of v1, /device:TPU:25, one launch (start us, length us, event | category | flops | bytes accessed | tf_op | source)
XLA Modules:
  0.0 53.6 jit_solution(8583685189860704956)
XLA Ops:
  0.0 0.7 %dynamic_slice.6 = s32[4]{0:T(128)S(1)} dynamic-slice(s32[64]{0:T(128)} %param.11, s32[]{:T(128)S(6)} %select_n.4), dynamic_slice_sizes={4} | dynamic-slice | bytes 36 | tf_op jit(solution)/shard_map/dynamic_slice | solution.py:194
  0.7 0.7 %dynamic_slice.7 = s32[4]{0:T(128)S(1)} dynamic-slice(s32[64]{0:T(128)} %param.12, s32[]{:T(128)S(6)} %select_n.4), dynamic_slice_sizes={4} | dynamic-slice | bytes 36 | tf_op jit(solution)/shard_map/dynamic_slice | solution.py:195
  1.5 0.7 %broadcast_multiply_fusion = s32[64]{0:T(128)S(1)} fusion(s32[64]{0:T(128)} %param.12), kind=kLoop, calls=%fused_computation.2 | loop fusion | flops 64 | bytes 512 | tf_op jit(solution)/shard_map/mul | solution.py:201
  2.1 0.7 %broadcast_in_dim.13 = s32[16,4]{1,0:T(8,128)S(1)} reshape(s32[64]{0:T(128)} %param.11) | data formatting | bytes 512 | tf_op jit(solution)/shard_map/broadcast_in_dim | solution.py:205
  2.9 0.1 stack_reshape.19
  3.0 0.1 iota_add_fusion
  3.1 0.1 add.50
  3.2 0.1 broadcast_in_dim.12
  3.2 0.1 stack_reshape.18
  3.4 0.1 stack_reshape.17
  3.5 0.7 %broadcast_in_dim.10 = s32[64,4]{1,0:T(8,128)S(1)} broadcast(s32[64]{0:T(128)} %param.12), dimensions={0} | broadcast | bytes 1280 | tf_op jit(solution)/shard_map/broadcast_in_dim | solution.py:202
  4.2 0.1 stack_reshape.16
  4.3 0.1 reshape.128
  4.5 0.0 copy-start
  4.5 0.8 %copy.12.mc_ref = s32[256,8]{1,0:T(8,128)} copy(s32[256,8]{0,1:T(8,128)S(1)} %bitcast.5) | data formatting | bytes 16384 | tf_op jit(solution)/shard_map/transpose | solution.py:211
  5.3 1.7 %reshape.121.x_ref = bf16[256,512]{1,0:T(8,128)(2,1)} reshape(bf16[64,4,512]{2,1,0:T(4,128)(2,1)} %param.10) | data formatting | bytes 524288 | tf_op jit(solution)/shard_map/reshape | solution.py:243
  7.0 0.0 copy-done
  7.0 44.9 %shard_map.100 = bf16[256,512]{1,0:T(8,128)(2,1)} custom-call(bf16[256,512]{1,0:T(8,128)(2,1)} %reshape.121.x_ref, s32[256,8]{1,0:T(8,128)} %copy.12.mc_ref, s32[8,256]{1,0:T(8,128)} %copy-done, f32[1,512]{1,0:T(1,128)} %bitcast.6, bf16[512,1536]{1,0:T(8,128)(2,1)} %w_qkv_ref.1, bf16[512,512]{1,0:T(8,128)(2,1)} %w_out_ref.1, f32[1,512]{1,0:T(1,128)} %bitcast.7, ...), custom_call_target="tpu_custom_call" | custom-call | tf_op jit(solution)/shard_map/pallas_call | solution.py:218
  51.9 1.7 %copy.14 = bf16[4,64,512]{2,1,0:T(8,128)(2,1)} copy(bf16[4,64,512]{2,1,0:T(8,128)(2,1)} %bitcast.4) | data formatting | bytes 524288
  (4 shorter events, 0.1 us)
Async XLA Ops:
  4.5 2.5 %copy-start = (s32[8,256]{1,0:T(8,128)}, s32[8,256]{1,0:T(8,128)S(1)}, u32[]{:S(2)}) copy-start(s32[8,256]{1,0:T(8,128)S(1)} %stack.3.mr_ref) | copy-start | bytes 24580

commit v2 on v1

--- a/solution.py
+++ b/solution.py
@@ -47,16 +47,19 @@
 
 
 def kernel(
-    n, x_ref, mc_ref, mr_ref, gain_a_ref, w_qkv_ref, w_out_ref, gain_f_ref, gate_ref, up_ref, down_ref,
-    out_ref, sent, ell_out, q_buf, k_buf, v_buf, got, got_ell, attn_m, gu, dn,
-    sx_send, sx_recv, sa_send, sa_recv, z_send, z_recv, x_send, x_recv, c_send, c_recv,
+    n, x_ref, col_ref, row_ref, gain_a_ref, w_qkv_ref, w_out_ref, gain_f_ref, gate_ref, up_ref, down_ref,
+    out_ref, mc_ref, mr_ref, sent, ell_out, q_buf, k_buf, v_buf, got, got_ell, attn_m, gu, dn,
+    sx_send, sx_recv, sa_send, sa_recv, z_send, z_recv, x_send, x_recv, y_send, y_recv, c_send, c_recv,
 ):
     me = lax.axis_index("harm")
+    sample = lax.axis_index("sample")
+    part = sample % 2
+    other_plane = {"sample": sample + 1 - 2 * part, "harm": me}
     outer = n // 4
     zc, inner = me // 4, me % 4
     side, core = inner // 2, inner % 2
-    other_side = zc * 4 + (1 - side) * 2 + core
-    other_core = zc * 4 + side * 2 + (1 - core)
+    other_side = {"harm": zc * 4 + (1 - side) * 2 + core}
+    other_core = {"harm": zc * 4 + side * 2 + (1 - core)}
     depth = gate_ref.shape[0]
     deep = down_ref.shape[0]
     tokens, width = x_ref.shape
@@ -70,13 +73,52 @@
     barrier = pltpu.get_barrier_semaphore()
     for d in range(1, n):
         pl.semaphore_signal(barrier, inc=1, device_id={"harm": (me + d) % n}, device_id_type=MESH)
+    pl.semaphore_signal(barrier, inc=1, device_id=other_plane, device_id_type=MESH)
+
+    length = col_ref.shape[1]
+    cols, rows_here = tokens // length, length // n
+    low_bits, mid_bits = cols.bit_length() - 1, rows_here.bit_length() - 1
+    wide = lax.broadcasted_iota(jnp.int32, (length, length), 1)
+    tall = lax.broadcasted_iota(jnp.int32, (length, length), 0)
+
+    def upright(ref):
+        return jnp.sum(jnp.where(wide == tall, ref[...].astype(jnp.float32), 0.0), axis=1, keepdims=True)
+
+    def slots(shape, axis):
+        t = lax.broadcasted_iota(jnp.int32, shape, axis)
+        c = t & (cols - 1)
+        source = t >> (low_bits + mid_bits)
+        row = (t >> low_bits) & (rows_here - 1)
+        return [t >> low_bits, me * cols + c, me * rows_here + row, source * cols + c]
+
+    def fields(axis):
+        shape = (tokens, length) if axis == 0 else (length, tokens)
+        lists = (row_ref, col_ref, row_ref, col_ref)
+        which = lax.broadcasted_iota(jnp.int32, shape, 1 - axis)
+        out = []
+        for ref, slot in zip(lists, slots(shape, axis)):
+            values = ref[...].astype(jnp.float32) if axis == 0 else upright(ref)
+            picked = jnp.where(which == slot, values, 0.0)
+            out.append(jnp.sum(picked, axis=1 - axis, keepdims=True).astype(jnp.int32))
+        return out
+
+    for k, value in enumerate(fields(0)):
+        mc_ref[:, k + 1 : k + 2] = value
+    for k, value in enumerate(fields(1)):
+        mr_ref[k + 1 : k + 2, :] = value
+    t = lax.broadcasted_iota(jnp.int32, (tokens, 1), 0)
+    mc_ref[:, 0:1] = mc_ref[:, 1:2] * cols + (t & (cols - 1))
+    in_row = t & (length - 1)
+    source = in_row >> low_bits
+    row = t >> (length.bit_length() - 1)
+    mc_ref[:, 5:6] = (source << (low_bits + mid_bits)) + (row << low_bits) + (in_row & (cols - 1))
 
     gu[0, pl.ds(pl.multiple_of(me * depth, depth), depth), :] = gate_ref[...]
     gu[1, pl.ds(pl.multiple_of(me * depth, depth), depth), :] = up_ref[...]
     dn[pl.ds(pl.multiple_of(me * deep, deep), deep), :] = down_ref[...]
     sent[...] = dot(one_hot_rows(mc_ref[:, 0:1], tokens), x_ref[...]).astype(jnp.bfloat16)
 
-    pl.semaphore_wait(barrier, n - 1)
+    pl.semaphore_wait(barrier, n)
 
     def rows_of(ref, i):
         return ref.at[pl.ds(pl.multiple_of(i * block, block), block), :]
@@ -88,16 +130,23 @@
             device_id={"harm": peer}, device_id_type=MESH,
         )
 
-    def shard(i, send, recv, slot, device):
-        first = gu.at[:, pl.ds(pl.multiple_of(i * depth, depth), depth), :]
-        second = dn.at[pl.ds(pl.multiple_of(i * deep, deep), deep), :]
-        return [
-            pltpu.make_async_remote_copy(
-                src_ref=ref, dst_ref=ref, send_sem=send.at[slot, k], recv_sem=recv.at[slot, k],
-                device_id={"harm": device}, device_id_type=MESH,
+    def shard(i, half, send, recv, slot, device):
+        copies = []
+        for k, ref in enumerate((gu, dn)):
+            size = (depth, deep)[k]
+            first, rows = i * size, size
+            if half is not None:
+                rows = size // 2
+                first = first + half * rows
+            where = pl.ds(pl.multiple_of(first, rows), rows)
+            piece = ref.at[:, where, :] if k == 0 else ref.at[where, :]
+            copies.append(
+                pltpu.make_async_remote_copy(
+                    src_ref=piece, dst_ref=piece, send_sem=send.at[slot, k], recv_sem=recv.at[slot, k],
+                    device_id=device, device_id_type=MESH,
+                )
             )
-            for k, ref in enumerate((first, second))
-        ]
+        return copies
 
     def place(d, s, c):
         return ((zc + outer - d) % outer) * 4 + s * 2 + c
@@ -109,11 +158,15 @@
             copy.start()
         pending.extend(copies)
 
+    def arrived(copies):
+        for copy in copies:
+            copy.wait_recv()
+
     start([to_row(sent, got, sx_send, sx_recv, d) for d in range(1, n)])
     for d in range(1, outer):
-        start(shard(me, z_send, z_recv, d, ((zc + d) % outer) * 4 + inner))
-    start(shard(me, x_send, x_recv, 0, other_side))
-    start(shard(me, c_send, c_recv, 0, other_core))
+        start(shard(me, part, z_send, z_recv, d, {"harm": ((zc + d) % outer) * 4 + inner}))
+    start(shard(me, part, x_send, x_recv, 0, other_side))
+    start(shard(me, None, c_send, c_recv, 0, other_core))
     rows_of(got, me)[...] = rows_of(sent, me)[...]
 
     def project(source, first):
@@ -147,10 +200,10 @@
 
     for d in range(1, outer):
         i = place(d, side, core)
-        for copy in shard(i, z_send, z_recv, d, me):
-            copy.wait_recv()
-        start(shard(i, x_send, x_recv, d, other_side))
-        start(shard(i, c_send, c_recv, d, other_core))
+        arrived(shard(i, part, z_send, z_recv, d, other_core))
+        start(shard(i, part, x_send, x_recv, d, other_side))
+        start(shard(i, part, y_send, y_recv, d, other_plane))
+        start(shard(i, part, c_send, c_recv, d, other_core))
 
     for d in range(1, n):
         to_row(sent, got, sx_send, sx_recv, d).wait_recv()
@@ -159,9 +212,14 @@
 
     for d in range(outer):
         i = place(d, 1 - side, core)
-        for copy in shard(i, x_send, x_recv, d, me):
-            copy.wait_recv()
-        start(shard(i, c_send, c_recv, outer + d, other_core))
+        arrived(shard(i, part, x_send, x_recv, d, other_side))
+        start(shard(i, part, y_send, y_recv, outer + d, other_plane))
+        start(shard(i, part, c_send, c_recv, outer + d, other_core))
+
+    for slot in range(1, 2 * outer):
+        i = place(slot % outer, side if slot < outer else 1 - side, core)
+        arrived(shard(i, 1 - part, y_send, y_recv, slot, other_plane))
+        start(shard(i, 1 - part, c_send, c_recv, 2 * outer + slot, other_core))
 
     for d in range(1, n):
         to_row(ell_out, got_ell, sa_send, sa_recv, d).wait_recv()
@@ -170,10 +228,11 @@
     )
     normed_ffn = rms_scale(resid, gain_f_ref[...]).astype(jnp.bfloat16)
 
-    for slot in range(2 * outer):
+    arrived(shard(place(0, side, 1 - core), None, c_send, c_recv, 0, other_core))
+    for slot in range(1, 2 * outer):
         i = place(slot % outer, side if slot < outer else 1 - side, 1 - core)
-        for copy in shard(i, c_send, c_recv, slot, me):
-            copy.wait_recv()
+        arrived(shard(i, part, c_send, c_recv, slot, other_core))
+        arrived(shard(i, 1 - part, c_send, c_recv, 2 * outer + slot, other_core))
     gate = dot(normed_ffn, gu[0])
     up = dot(normed_ffn, gu[1])
     hidden = (gate / (1.0 + jnp.exp(-gate)) * up).astype(jnp.bfloat16)
@@ -186,30 +245,11 @@
 
 
 def per_device(n, inputs, col_list, row_list, gain_attn, w_qkv, w_out, gain_ffn, w_gate, w_up, w_down):
-    place = lax.axis_index("harm")
     length, cols, width = inputs.shape
     rows_here = length // n
     tokens = length * cols
     split = width // 2
-    my_cols = lax.dynamic_slice_in_dim(col_list, place * cols, cols)
-    my_rows = lax.dynamic_slice_in_dim(row_list, place * rows_here, rows_here)
-    before, after = (length, cols), (n, rows_here, cols)
-    slot = jnp.arange(cols, dtype=jnp.int32)
-    order = jnp.arange(tokens, dtype=jnp.int32).reshape(n, rows_here, cols).transpose(0, 1, 2)
-    back = order.transpose(1, 0, 2)
-    table = [
-        jnp.broadcast_to(row_list[:, None] * cols + slot[None, :], before),
-        jnp.broadcast_to(row_list[:, None], before),
-        jnp.broadcast_to(my_cols[None, :], before),
-        jnp.broadcast_to(my_rows[None, :, None], after),
-        jnp.broadcast_to(col_list.reshape(n, 1, cols), after),
-        back,
-        back,
-        back,
-    ]
-    by_row = jnp.stack([entry.reshape(tokens) for entry in table], axis=0)
-    by_col = by_row.T
-    bf16, f32 = jnp.bfloat16, jnp.float32
+    bf16 = jnp.bfloat16
     depth, ff = w_gate.shape
     deep = w_down.shape[0]
     outer = n // 4
@@ -221,6 +261,8 @@
         in_specs=[vmem] * 10,
         out_specs=vmem,
         scratch_shapes=[
+            pltpu.VMEM((tokens, 8), jnp.int32),
+            pltpu.VMEM((8, tokens), jnp.int32),
             pltpu.VMEM((tokens, width), bf16),
             pltpu.VMEM((tokens, split), bf16),
             pltpu.VMEM((tokens, split), bf16),
@@ -235,12 +277,13 @@
             dma((outer, 2)), dma((outer, 2)),
             dma((outer, 2)), dma((outer, 2)),
             dma((2 * outer, 2)), dma((2 * outer, 2)),
+            dma((4 * outer, 2)), dma((4 * outer, 2)),
         ],
         compiler_params=pltpu.CompilerParams(
             collective_id=0, has_side_effects=True, vmem_limit_bytes=56 * 1024 * 1024
         ),
     )(
-        inputs.reshape(tokens, width), by_col, by_row, gain_attn.reshape(1, width), w_qkv, w_out,
+        inputs.reshape(tokens, width), col_list.reshape(1, length), row_list.reshape(1, length), gain_attn.reshape(1, width), w_qkv, w_out,
         gain_ffn.reshape(1, width), w_gate, w_up, w_down,
     )
     return result.reshape(rows_here, length, width)

time: 53.8 us -> 45.9 us (0.85)
  the two profiles are of different devices: /device:TPU:25 before, /device:TPU:1 now
where the time goes in v2:
time: 45.9 us; the launch traced here: 45.7 us
  Pallas kernels  42.3 us (92%)
  local copies, waits for them, and re-layouts  3.39 us (7%)
    pallas_call x1, Pallas kernels, per_device(): pl.pallas_call(functools.partial(kernel, n), out_shape=jax.ShapeDtypeStru...  42.3 us
    reshape x1, local copies, waits for them, and re-layouts, per_device(): inputs.reshape(tokens, width)  1.72 us
    unnamed x1, local copies, waits for them, and re-layouts  1.67 us

profile of v2, /device:TPU:1, one launch (start us, length us, event | category | flops | bytes accessed | tf_op | source)
XLA Modules:
  0.0 45.7 jit_solution(1492161977453331188)
XLA Ops:
  0.0 1.7 %reshape.18.x_ref = bf16[256,512]{1,0:T(8,128)(2,1)} reshape(bf16[64,4,512]{2,1,0:T(4,128)(2,1)} %param.10) | data formatting | bytes 524288 | tf_op jit(solution)/shard_map/reshape | solution.py:286
  1.7 42.3 %shard_map.100 = bf16[256,512]{1,0:T(8,128)(2,1)} custom-call(bf16[256,512]{1,0:T(8,128)(2,1)} %reshape.18.x_ref, s32[1,64]{1,0:T(1,128)} %bitcast.8, s32[1,64]{1,0:T(1,128)} %bitcast.9, f32[1,512]{1,0:T(1,128)} %bitcast.6, bf16[512,1536]{1,0:T(8,128)(2,1)} %w_qkv_ref.1, bf16[512,512]{1,0:T(8,128)(2,1)} %w_out_ref.1, f32[1,512]{1,0:T(1,128)} %bitcast.7, ...), custom_call_target="tpu_custom_call" | custom-call | tf_op jit(solution)/shard_map/pallas_call | solution.py:258
  44.0 1.7 %copy.12 = bf16[4,64,512]{2,1,0:T(8,128)(2,1)} copy(bf16[4,64,512]{2,1,0:T(8,128)(2,1)} %bitcast.5) | data formatting | bytes 524288

commit v3 on v2

--- a/solution.py
+++ b/solution.py
@@ -130,12 +130,15 @@
             device_id={"harm": peer}, device_id_type=MESH,
         )
 
-    def shard(i, half, send, recv, slot, device):
+    def pieces(i, halves, send, recv, slot, device):
         copies = []
         for k, ref in enumerate((gu, dn)):
+            half = halves[k]
+            if half is None:
+                continue
             size = (depth, deep)[k]
             first, rows = i * size, size
-            if half is not None:
+            if half is not whole:
                 rows = size // 2
                 first = first + half * rows
             where = pl.ds(pl.multiple_of(first, rows), rows)
@@ -148,25 +151,99 @@
             )
         return copies
 
-    def place(d, s, c):
-        return ((zc + outer - d) % outer) * 4 + s * 2 + c
+    whole = "all"
+    full, mine, theirs = (whole, whole), (part, whole), (1 - part, None)
+    traded = (part, None)
+
+    def place(z, s, c):
+        return z * 4 + s * 2 + c
 
     pending = []
 
-    def start(copies):
-        for copy in copies:
-            copy.start()
-        pending.extend(copies)
-
-    def arrived(copies):
-        for copy in copies:
-            copy.wait_recv()
-
-    start([to_row(sent, got, sx_send, sx_recv, d) for d in range(1, n)])
-    for d in range(1, outer):
-        start(shard(me, part, z_send, z_recv, d, {"harm": ((zc + d) % outer) * 4 + inner}))
-    start(shard(me, part, x_send, x_recv, 0, other_side))
-    start(shard(me, None, c_send, c_recv, 0, other_core))
+    def guard(cond, body):
+        if cond is None:
+            body()
+        else:
+            pl.when(cond)(body)
+
+    def start(build, cond=None):
+        def body():
+            for copy in build():
+                copy.start()
+
+        guard(cond, body)
+        pending.append((cond, build))
+
+    def arrived(build, cond=None):
+        def body():
+            for copy in build():
+                copy.wait_recv()
+
+        guard(cond, body)
+
+    def send(cond, *args):
+        start(lambda: pieces(*args), cond)
+
+    def receive(cond, *args):
+        arrived(lambda: pieces(*args), cond)
+
+    def both(a, b):
+        return b if a is None else a & b
+
+    def reached(t):
+        if t == 0:
+            return [(zc, None, 0)]
+        return [(zc - t, zc - t >= 0, 0), (zc + t, zc + t < outer, 1)]
+
+    def along_z(t, z, cond, stream):
+        step_z = 1 - 2 * stream
+        ahead = zc + step_z
+        ok = both(cond, (ahead < outer) if stream == 0 else (ahead >= 0))
+        if t + 1 < outer:
+            device = {"harm": ahead * 4 + inner}
+            send(ok, place(z, side, core), mine, z_send, z_recv, stream * outer + t + 1, device)
+
+    def z_stage(t):
+        for z, cond, stream in reached(t):
+            i = place(z, side, core)
+            receive(cond, i, mine, z_send, z_recv, stream * outer + t, other_core)
+            along_z(t, z, cond, stream)
+            send(cond, i, mine, x_send, x_recv, z, other_side)
+            send(cond, i, traded, y_send, y_recv, z, other_plane)
+            send(cond, i, mine, c_send, c_recv, z, other_core)
+
+    def x_stage(t):
+        for z, cond, stream in reached(t):
+            i = place(z, 1 - side, core)
+            receive(cond, i, mine, x_send, x_recv, z, other_side)
+            send(cond, i, traded, y_send, y_recv, outer + z, other_plane)
+            send(cond, i, mine, c_send, c_recv, outer + z, other_core)
+
+    def y_stage(t, other):
+        for z, cond, stream in reached(t):
+            i = place(z, 1 - side if other else side, core)
+            slot = outer * other + z
+            receive(cond, i, theirs, y_send, y_recv, slot, other_plane)
+            send(cond, i, theirs, c_send, c_recv, 2 * outer + slot, other_core)
+
+    def core_stage(t, other):
+        for z, cond, stream in reached(t):
+            i = place(z, 1 - side if other else side, 1 - core)
+            slot = outer * other + z
+            if t == 0 and not other:
+                receive(None, i, full, c_send, c_recv, slot, other_core)
+            else:
+                receive(cond, i, mine, c_send, c_recv, slot, other_core)
+                receive(cond, i, theirs, c_send, c_recv, 2 * outer + slot, other_core)
+
+    def tokens_out(src, dst, send_sem, recv_sem):
+        return lambda: [to_row(src, dst, send_sem, recv_sem, d) for d in range(1, n)]
+
+    for stream in (0, 1):
+        along_z(0, zc, None, stream)
+    send(None, me, mine, x_send, x_recv, zc, other_side)
+    send(None, me, full, c_send, c_recv, zc, other_core)
+    start(tokens_out(sent, got, sx_send, sx_recv))
     rows_of(got, me)[...] = rows_of(sent, me)[...]
 
     def project(source, first):
@@ -194,45 +271,33 @@
         lax.fori_loop(0, tokens // step, body, 0)
 
     project(sent, 0)
+    z_stage(1)
     attend(ell_out, 2, 1, True)
-    start([to_row(ell_out, got_ell, sa_send, sa_recv, d) for d in range(1, n)])
+    start(tokens_out(ell_out, got_ell, sa_send, sa_recv))
     rows_of(got_ell, me)[...] = rows_of(ell_out, me)[...]
 
-    for d in range(1, outer):
-        i = place(d, side, core)
-        arrived(shard(i, part, z_send, z_recv, d, other_core))
-        start(shard(i, part, x_send, x_recv, d, other_side))
-        start(shard(i, part, y_send, y_recv, d, other_plane))
-        start(shard(i, part, c_send, c_recv, d, other_core))
-
-    for d in range(1, n):
-        to_row(sent, got, sx_send, sx_recv, d).wait_recv()
+    x_stage(0)
+    for t in range(2, outer):
+        z_stage(t)
+        x_stage(t - 1)
+    y_stage(0, 1)
+    arrived(tokens_out(sent, got, sx_send, sx_recv))
     project(got, split)
+    x_stage(outer - 1)
     attend(attn_m, 4, 3, False)
-
-    for d in range(outer):
-        i = place(d, 1 - side, core)
-        arrived(shard(i, part, x_send, x_recv, d, other_side))
-        start(shard(i, part, y_send, y_recv, outer + d, other_plane))
-        start(shard(i, part, c_send, c_recv, outer + d, other_core))
-
-    for slot in range(1, 2 * outer):
-        i = place(slot % outer, side if slot < outer else 1 - side, core)
-        arrived(shard(i, 1 - part, y_send, y_recv, slot, other_plane))
-        start(shard(i, 1 - part, c_send, c_recv, 2 * outer + slot, other_core))
-
-    for d in range(1, n):
-        to_row(ell_out, got_ell, sa_send, sa_recv, d).wait_recv()
+    for t in range(1, outer):
+        y_stage(t, 0)
+        y_stage(t, 1)
+
+    arrived(tokens_out(ell_out, got_ell, sa_send, sa_recv))
     resid = got[...].astype(jnp.float32) + (
         dot(got_ell[...], w_out_ref[:split, :]) + dot(attn_m[...], w_out_ref[split:, :])
     )
     normed_ffn = rms_scale(resid, gain_f_ref[...]).astype(jnp.bfloat16)
 
-    arrived(shard(place(0, side, 1 - core), None, c_send, c_recv, 0, other_core))
-    for slot in range(1, 2 * outer):
-        i = place(slot % outer, side if slot < outer else 1 - side, 1 - core)
-        arrived(shard(i, part, c_send, c_recv, slot, other_core))
-        arrived(shard(i, 1 - part, c_send, c_recv, 2 * outer + slot, other_core))
+    for t in range(outer):
+        for other in (0, 1):
+            core_stage(t, other)
     gate = dot(normed_ffn, gu[0])
     up = dot(normed_ffn, gu[1])
     hidden = (gate / (1.0 + jnp.exp(-gate)) * up).astype(jnp.bfloat16)
@@ -240,8 +305,13 @@
     valid = mc_ref[:, 4:5] <= mc_ref[:, 3:4]
     final = jnp.where(valid, final, 0.0).astype(jnp.bfloat16)
     out_ref[...] = dot(one_hot_rows(mc_ref[:, 5:6], tokens), final).astype(jnp.bfloat16)
-    for copy in pending:
-        copy.wait_send()
+    for cond, build in pending:
+
+        def finish(build=build):
+            for copy in build():
+                copy.wait_send()
+
+        guard(cond, finish)
 
 
 def per_device(n, inputs, col_list, row_list, gain_attn, w_qkv, w_out, gain_ffn, w_gate, w_up, w_down):
@@ -274,7 +344,7 @@
             pltpu.VMEM((2, depth * n, ff), bf16),
             pltpu.VMEM((deep * n, width), bf16),
             dma((n,)), dma((n,)), dma((n,)), dma((n,)),
-            dma((outer, 2)), dma((outer, 2)),
+            dma((2 * outer, 2)), dma((2 * outer, 2)),
             dma((outer, 2)), dma((outer, 2)),
             dma((2 * outer, 2)), dma((2 * outer, 2)),
             dma((4 * outer, 2)), dma((4 * outer, 2)),

time: 45.9 us -> 41.4 us (0.902)
  Pallas kernels: 42.3 us -> 37.8 us
    pallas_call x1, Pallas kernels: 42.3 us -> 37.8 us  [per_device(): pl.pallas_call(functools.partial(kernel, n), out_shape=jax.ShapeDtypeStru...]
where the time goes in v3:
time: 41.4 us; the launch traced here: 41.2 us
  Pallas kernels  37.8 us (91%)
  local copies, waits for them, and re-layouts  3.39 us (8%)
    pallas_call x1, Pallas kernels, per_device(): pl.pallas_call(functools.partial(kernel, n), out_shape=jax.ShapeDtypeStru...  37.8 us
    reshape x1, local copies, waits for them, and re-layouts, per_device(): inputs.reshape(tokens, width)  1.72 us
    unnamed x1, local copies, waits for them, and re-layouts  1.67 us

profile of v3, /device:TPU:1, one launch (start us, length us, event | category | flops | bytes accessed | tf_op | source)
XLA Modules:
  0.0 41.2 jit_solution(12861736867135604507)
XLA Ops:
  0.0 1.7 %reshape.18.x_ref = bf16[256,512]{1,0:T(8,128)(2,1)} reshape(bf16[64,4,512]{2,1,0:T(4,128)(2,1)} %param.10) | data formatting | bytes 524288 | tf_op jit(solution)/shard_map/reshape | solution.py:356
  1.7 37.8 %shard_map.100 = bf16[256,512]{1,0:T(8,128)(2,1)} custom-call(bf16[256,512]{1,0:T(8,128)(2,1)} %reshape.18.x_ref, s32[1,64]{1,0:T(1,128)} %bitcast.8, s32[1,64]{1,0:T(1,128)} %bitcast.9, f32[1,512]{1,0:T(1,128)} %bitcast.6, bf16[512,1536]{1,0:T(8,128)(2,1)} %w_qkv_ref.1, bf16[512,512]{1,0:T(8,128)(2,1)} %w_out_ref.1, f32[1,512]{1,0:T(1,128)} %bitcast.7, ...), custom_call_target="tpu_custom_call" | custom-call | tf_op jit(solution)/shard_map/pallas_call | solution.py:328
  39.6 1.7 %copy.12 = bf16[4,64,512]{2,1,0:T(8,128)(2,1)} copy(bf16[4,64,512]{2,1,0:T(8,128)(2,1)} %bitcast.5) | data formatting | bytes 524288

commit v4 on v3

--- a/solution.py
+++ b/solution.py
@@ -47,8 +47,8 @@
 
 
 def kernel(
-    n, x_ref, col_ref, row_ref, gain_a_ref, w_qkv_ref, w_out_ref, gain_f_ref, gate_ref, up_ref, down_ref,
-    out_ref, mc_ref, mr_ref, sent, ell_out, q_buf, k_buf, v_buf, got, got_ell, attn_m, gu, dn,
+    n, x_ref, col_ref, row_ref, gain_a_ref, w_qkv_hbm, w_out_hbm, gain_f_ref, gate_ref, up_ref, down_ref,
+    out_ref, w_qkv_ref, w_out_ref, w_sem, mc_ref, mr_ref, sent, ell_out, q_buf, k_buf, v_buf, got, got_ell, attn_m, gu, dn,
     sx_send, sx_recv, sa_send, sa_recv, z_send, z_recv, x_send, x_recv, y_send, y_recv, c_send, c_recv,
 ):
     me = lax.axis_index("harm")
@@ -62,7 +62,7 @@
     other_core = {"harm": zc * 4 + side * 2 + (1 - core)}
     depth = gate_ref.shape[0]
     deep = down_ref.shape[0]
-    tokens, width = x_ref.shape
+    tokens, width = x_ref.shape[0] * x_ref.shape[1], x_ref.shape[2]
     block = tokens // n
     split = width // 2
     head_dim = width // HEADS
@@ -70,6 +70,10 @@
     scale = head_dim ** (-0.5)
     step = min(tokens, 256)
 
+    fetch_qkv = pltpu.make_async_copy(w_qkv_hbm, w_qkv_ref, w_sem.at[0])
+    fetch_out = pltpu.make_async_copy(w_out_hbm, w_out_ref, w_sem.at[1])
+    fetch_qkv.start()
+    fetch_out.start()
     barrier = pltpu.get_barrier_semaphore()
     for d in range(1, n):
         pl.semaphore_signal(barrier, inc=1, device_id={"harm": (me + d) % n}, device_id_type=MESH)
@@ -116,7 +120,7 @@
     gu[0, pl.ds(pl.multiple_of(me * depth, depth), depth), :] = gate_ref[...]
     gu[1, pl.ds(pl.multiple_of(me * depth, depth), depth), :] = up_ref[...]
     dn[pl.ds(pl.multiple_of(me * deep, deep), deep), :] = down_ref[...]
-    sent[...] = dot(one_hot_rows(mc_ref[:, 0:1], tokens), x_ref[...]).astype(jnp.bfloat16)
+    sent[...] = dot(one_hot_rows(mc_ref[:, 0:1], tokens), x_ref[...].reshape(tokens, width)).astype(jnp.bfloat16)
 
     pl.semaphore_wait(barrier, n)
 
@@ -152,8 +156,8 @@
         return copies
 
     whole = "all"
-    full, mine, theirs = (whole, whole), (part, whole), (1 - part, None)
-    traded = (part, None)
+    full, mine, theirs = (whole, whole), (part, part), (1 - part, 1 - part)
+    traded = (part, part)
 
     def place(z, s, c):
         return z * 4 + s * 2 + c
@@ -270,6 +274,7 @@
 
         lax.fori_loop(0, tokens // step, body, 0)
 
+    fetch_qkv.wait()
     project(sent, 0)
     z_stage(1)
     attend(ell_out, 2, 1, True)
@@ -290,6 +295,7 @@
         y_stage(t, 1)
 
     arrived(tokens_out(ell_out, got_ell, sa_send, sa_recv))
+    fetch_out.wait()
     resid = got[...].astype(jnp.float32) + (
         dot(got_ell[...], w_out_ref[:split, :]) + dot(attn_m[...], w_out_ref[split:, :])
     )
@@ -324,13 +330,17 @@
     deep = w_down.shape[0]
     outer = n // 4
     vmem = pl.BlockSpec(memory_space=pltpu.VMEM)
+    hbm = pl.BlockSpec(memory_space=pl.ANY)
     dma = pltpu.SemaphoreType.DMA
     result = pl.pallas_call(
         functools.partial(kernel, n),
         out_shape=jax.ShapeDtypeStruct((tokens, width), bf16),
-        in_specs=[vmem] * 10,
+        in_specs=[vmem] * 4 + [hbm] * 2 + [vmem] * 4,
         out_specs=vmem,
         scratch_shapes=[
+            pltpu.VMEM(w_qkv.shape, bf16),
+            pltpu.VMEM(w_out.shape, bf16),
+            dma((2,)),
             pltpu.VMEM((tokens, 8), jnp.int32),
             pltpu.VMEM((8, tokens), jnp.int32),
             pltpu.VMEM((tokens, width), bf16),
@@ -353,7 +363,7 @@
             collective_id=0, has_side_effects=True, vmem_limit_bytes=56 * 1024 * 1024
         ),
     )(
-        inputs.reshape(tokens, width), col_list.reshape(1, length), row_list.reshape(1, length), gain_attn.reshape(1, width), w_qkv, w_out,
+        inputs, col_list.reshape(1, length), row_list.reshape(1, length), gain_attn.reshape(1, width), w_qkv, w_out,
         gain_ffn.reshape(1, width), w_gate, w_up, w_down,
     )
     return result.reshape(rows_here, length, width)

time: 41.4 us -> 37.4 us (0.903)
  Pallas kernels: 37.8 us -> 35.5 us
  local copies, waits for them, and re-layouts: 3.39 us -> 1.67 us
    pallas_call x1, Pallas kernels: 37.8 us -> 35.5 us  [per_device(): pl.pallas_call(functools.partial(kernel, n), out_shape=jax.ShapeDtypeStru...]
    reshape x1 -> x0, local copies, waits for them, and re-layouts: 1.72 us -> none  [per_device(): inputs.reshape(tokens, width)]
where the time goes in v4:
time: 37.4 us; the launch traced here: 37.2 us
  Pallas kernels  35.5 us (95%)
  local copies, waits for them, and re-layouts  1.67 us (4%)
    pallas_call x1, Pallas kernels, per_device(): pl.pallas_call(functools.partial(kernel, n), out_shape=jax.ShapeDtypeStru...  35.5 us
    unnamed x1, local copies, waits for them, and re-layouts  1.67 us

profile of v4, /device:TPU:1, one launch (start us, length us, event | category | flops | bytes accessed | tf_op | source)
XLA Modules:
  0.0 37.2 jit_solution(11877853310639338695)
XLA Ops:
  0.0 35.5 %shard_map.100 = bf16[256,512]{1,0:T(8,128)(2,1)} custom-call(bf16[64,4,512]{2,1,0:T(4,128)(2,1)} %x_ref.1, s32[1,64]{1,0:T(1,128)} %bitcast.8, s32[1,64]{1,0:T(1,128)} %bitcast.9, f32[1,512]{1,0:T(1,128)} %bitcast.6, bf16[512,1536]{1,0:T(8,128)(2,1)} %w_qkv_hbm.1, bf16[512,512]{1,0:T(8,128)(2,1)} %w_out_hbm.1, f32[1,512]{1,0:T(1,128)} %bitcast.7, ...), custom_call_target="tpu_custom_call" | custom-call | tf_op jit(solution)/shard_map/pallas_call | solution.py:335
  35.5 1.7 %copy.12 = bf16[4,64,512]{2,1,0:T(8,128)(2,1)} copy(bf16[4,64,512]{2,1,0:T(8,128)(2,1)} %bitcast.5) | data formatting | bytes 524288

commit v5 on v4

--- a/solution.py
+++ b/solution.py
@@ -230,15 +230,18 @@
             receive(cond, i, theirs, y_send, y_recv, slot, other_plane)
             send(cond, i, theirs, c_send, c_recv, 2 * outer + slot, other_core)
 
-    def core_stage(t, other):
+    def core_stage(t, other, k):
+        def only(halves):
+            return tuple(half if j == k else None for j, half in enumerate(halves))
+
         for z, cond, stream in reached(t):
             i = place(z, 1 - side if other else side, 1 - core)
             slot = outer * other + z
             if t == 0 and not other:
-                receive(None, i, full, c_send, c_recv, slot, other_core)
+                receive(None, i, only(full), c_send, c_recv, slot, other_core)
             else:
-                receive(cond, i, mine, c_send, c_recv, slot, other_core)
-                receive(cond, i, theirs, c_send, c_recv, 2 * outer + slot, other_core)
+                receive(cond, i, only(mine), c_send, c_recv, slot, other_core)
+                receive(cond, i, only(theirs), c_send, c_recv, 2 * outer + slot, other_core)
 
     def tokens_out(src, dst, send_sem, recv_sem):
         return lambda: [to_row(src, dst, send_sem, recv_sem, d) for d in range(1, n)]
@@ -303,10 +306,13 @@
 
     for t in range(outer):
         for other in (0, 1):
-            core_stage(t, other)
+            core_stage(t, other, 0)
     gate = dot(normed_ffn, gu[0])
     up = dot(normed_ffn, gu[1])
     hidden = (gate / (1.0 + jnp.exp(-gate)) * up).astype(jnp.bfloat16)
+    for t in range(outer):
+        for other in (0, 1):
+            core_stage(t, other, 1)
     final = resid + dot(hidden, dn[...])
     valid = mc_ref[:, 4:5] <= mc_ref[:, 3:4]
     final = jnp.where(valid, final, 0.0).astype(jnp.bfloat16)

time: 37.4 us -> 37.5 us (level)
  no operation moved by 1% of the time
where the time goes in v5:
time: 37.5 us; the launch traced here: 37.3 us
  Pallas kernels  35.7 us (95%)
  local copies, waits for them, and re-layouts  1.67 us (4%)
    pallas_call x1, Pallas kernels, per_device(): pl.pallas_call(functools.partial(kernel, n), out_shape=jax.ShapeDtypeStru...  35.7 us
    unnamed x1, local copies, waits for them, and re-layouts  1.67 us

profile of v5, /device:TPU:1, one launch (start us, length us, event | category | flops | bytes accessed | tf_op | source)
XLA Modules:
  0.0 37.3 jit_solution(3752339222970054687)
XLA Ops:
  0.0 35.7 %shard_map.100 = bf16[256,512]{1,0:T(8,128)(2,1)} custom-call(bf16[64,4,512]{2,1,0:T(4,128)(2,1)} %x_ref.1, s32[1,64]{1,0:T(1,128)} %bitcast.8, s32[1,64]{1,0:T(1,128)} %bitcast.9, f32[1,512]{1,0:T(1,128)} %bitcast.6, bf16[512,1536]{1,0:T(8,128)(2,1)} %w_qkv_hbm.1, bf16[512,512]{1,0:T(8,128)(2,1)} %w_out_hbm.1, f32[1,512]{1,0:T(1,128)} %bitcast.7, ...), custom_call_target="tpu_custom_call" | custom-call | tf_op jit(solution)/shard_map/pallas_call | solution.py:341
  35.7 1.7 %copy.12 = bf16[4,64,512]{2,1,0:T(8,128)(2,1)} copy(bf16[4,64,512]{2,1,0:T(8,128)(2,1)} %bitcast.5) | data formatting | bytes 524288
